TPU v7x, 128 devices: a whole 4x4x4 slice. The times are simulated.
128 devices in a mesh: tensor: 8 (over y, core), adapter: 16 (over x, z).
Axes of the slice: x: 4, y: 4, z: 4, core: 2. Of those that a mesh axis runs over, the one named last changes fastest.
Arguments:
- tokens_in: bfloat16 [512, 8192], P(('tensor', 'adapter')), may hold values from -6 to 6
- w_gate: bfloat16 [8192, 28672], P(None, ('tensor', 'adapter')), may hold values from -0.0625 to 0.0625
- w_up: bfloat16 [8192, 28672], P(None, ('tensor', 'adapter')), may hold values from -0.0625 to 0.0625
- w_down: bfloat16 [28672, 8192], P('tensor', 'adapter'), may hold values from -0.03125 to 0.03125
- a_gate: bfloat16 [8192, 2048], P(None, 'adapter'), may hold values from -0.0625 to 0.0625
- a_up: bfloat16 [8192, 2048], P(None, 'adapter'), may hold values from -0.0625 to 0.0625
- b_gate: bfloat16 [2048, 28672], P(None, ('tensor', 'adapter')), may hold values from -1.5 to 1.5
- b_up: bfloat16 [2048, 28672], P(None, ('tensor', 'adapter')), may hold values from -1.5 to 1.5
- a_down: bfloat16 [28672, 2048], P(('tensor', 'adapter')), may hold values from -0.03125 to 0.03125
- b_down: bfloat16 [2048, 8192], P('adapter'), may hold values from -1.5 to 1.5
- lengths: int32 [8], replicated, may hold values from 1 to 128, 512 in all
- request_adapter: int32 [8], replicated, may hold values from 0 to 127
- placement: int32 [128], replicated, may hold values from 0 to 127, each once
Outputs:
- mixed: bfloat16 [512, 8192], P(('tensor', 'adapter'))
Inputs may be any that keep to these rules, and one draw needn't show every extreme that they name: The 8 lengths sum to 512; the longest is exactly 512 // 4. `placement`: each storage slot holds exactly one adapter.
All inputs are finite; a program needn't handle non-finite values.
Results may differ from a plain program's by a relative error of at most 0.0085.
Values may be sent and summed in bfloat16 or wider, within the bound.
No kernel may reach another device: no remote copies, remote signals or barrier semaphores. Data moves between devices by JAX's collectives and lax.ppermute only.
A program may use at most 128 MiB of HBM per device.

v0:
```python
import jax
import jax.numpy as jnp
from jax import lax
from jax.sharding import PartitionSpec as P

R = 16
ADP_DEV = 8


def token_tables(lengths, request_adapter, placement, all_tokens):
    positions = jnp.arange(all_tokens, dtype=jnp.int32)
    request_ends = jnp.cumsum(lengths)
    request = jnp.sum((positions[:, None] >= request_ends[None, :]).astype(jnp.int32), axis=1)
    request_hot = request[:, None] == jnp.arange(lengths.shape[0], dtype=jnp.int32)[None, :]
    adapter = jnp.sum(jnp.where(request_hot, request_adapter[None, :], 0), axis=1)
    adapter_hot = adapter[:, None] == jnp.arange(placement.shape[0], dtype=jnp.int32)[None, :]
    slot_index = jnp.sum(jnp.where(adapter_hot, placement[None, :], 0), axis=1)
    return (adapter_hot, slot_index)


def spread_block(low_rank, hot_rows):
    spread = jnp.where(
        hot_rows[:, :, None], low_rank[:, None, :], jnp.zeros_like(low_rank)[:, None, :]
    )
    return spread.reshape(low_rank.shape[0], -1)


def owner_shrink(rows_in, a_gate, a_up):
    return jnp.concatenate(
        [
            jnp.dot(rows_in, a_gate, preferred_element_type=jnp.float32),
            jnp.dot(rows_in, a_up, preferred_element_type=jnp.float32),
        ],
        axis=1,
    )


def local(
    tokens_in,
    w_gate,
    w_up,
    w_down,
    a_gate,
    a_up,
    b_gate,
    b_up,
    a_down,
    b_down,
    lengths,
    request_adapter,
    placement,
):
    n_tensor = lax.axis_size("tensor")
    n_adapter = lax.axis_size("adapter")
    tok_dev = tokens_in.shape[0]
    all_tokens = tok_dev * n_tensor * n_adapter
    group_rows = tok_dev * n_adapter
    adapter_count = placement.shape[0]
    adapter_hot, slot_index = token_tables(lengths, request_adapter, placement, all_tokens)
    group_start = lax.axis_index("tensor") * group_rows
    group_slot = lax.dynamic_slice_in_dim(slot_index, group_start, group_rows)
    owned = group_slot // ADP_DEV == lax.axis_index("adapter")
    local_mask = (group_slot % ADP_DEV)[:, None] == jnp.arange(ADP_DEV, dtype=jnp.int32)[None, :]
    keep_mask = owned[:, None] & local_mask
    rows_group = lax.all_gather(tokens_in, "adapter", axis=0, tiled=True)
    projected = owner_shrink(rows_group, a_gate, a_up).reshape(group_rows, 2, ADP_DEV, R)
    picked = jnp.sum(jnp.where(keep_mask[:, None, :, None], projected, 0.0), axis=2).reshape(
        group_rows, 2 * R
    )
    shrunk_group = lax.psum(picked, "adapter").astype(jnp.bfloat16)
    gathered, shrunk_all = (
        lax.all_gather(rows_group, "tensor", axis=0, tiled=True),
        lax.all_gather(shrunk_group, "tensor", axis=0, tiled=True),
    )
    gate_sum = jnp.dot(gathered, w_gate, preferred_element_type=jnp.float32) + jnp.dot(
        spread_block(shrunk_all[:, :R], adapter_hot), b_gate, preferred_element_type=jnp.float32
    )
    up_sum = jnp.dot(gathered, w_up, preferred_element_type=jnp.float32) + jnp.dot(
        spread_block(shrunk_all[:, R:], adapter_hot), b_up, preferred_element_type=jnp.float32
    )
    hidden = (jax.nn.silu(gate_sum) * up_sum).astype(jnp.bfloat16)
    down_all = jnp.dot(hidden, a_down, preferred_element_type=jnp.float32).reshape(
        all_tokens, adapter_count, R
    )
    low_part = jnp.sum(jnp.where(adapter_hot[:, :, None], down_all, 0.0), axis=1)
    down_full = lax.all_to_all(w_down, "adapter", split_axis=0, concat_axis=1, tiled=True)
    base_part = jnp.dot(hidden, down_full, preferred_element_type=jnp.float32)
    base_sum, low_sum = (
        lax.psum_scatter(base_part, ("tensor", "adapter"), scatter_dimension=0, tiled=True),
        lax.psum_scatter(low_part, ("tensor", "adapter"), scatter_dimension=0, tiled=True),
    )
    low_rank = low_sum.astype(jnp.bfloat16)
    low_group = lax.all_gather(low_rank, "adapter", axis=0, tiled=True)
    spread_low = jnp.where(
        keep_mask[:, :, None], low_group[:, None, :], jnp.zeros_like(low_group)[:, None, :]
    )
    spread_low = spread_low.reshape(group_rows, ADP_DEV * R)
    expanded = jnp.dot(spread_low, b_down, preferred_element_type=jnp.float32).astype(jnp.bfloat16)
    delta_down = lax.psum_scatter(
        expanded.astype(jnp.float32).astype(jnp.bfloat16),
        "adapter",
        scatter_dimension=0,
        tiled=True,
    ).astype(jnp.float32)
    return (base_sum + delta_down).astype(jnp.bfloat16)


def solution(mesh):
    in_specs = (
        P(("tensor", "adapter"), None),
        P(None, ("tensor", "adapter")),
        P(None, ("tensor", "adapter")),
        P("tensor", "adapter"),
        P(None, "adapter"),
        P(None, "adapter"),
        P(None, ("tensor", "adapter")),
        P(None, ("tensor", "adapter")),
        P(("tensor", "adapter"), None),
        P("adapter", None),
        P(),
        P(),
        P(),
    )
    out_specs = P(("tensor", "adapter"), None)
    return jax.shard_map(local, mesh=mesh, in_specs=in_specs, out_specs=out_specs, check_vma=False)
```

profile of v0, /device:TPU:1, one launch (start us, length us, event | category | flops | bytes accessed | tf_op | source)
XLA Modules:
  0.0 604.1 jit_solution(13579343601903260206)
XLA Ops:
  6.5 0.0 copy-start
  6.5 0.0 all-gather.8.cloned.1.call-start
  6.5 0.7 all-gather.8.cloned.1.call-update
  7.3 0.0 all-gather.6.cloned.1.call-start
  7.3 46.2 %all-gather.8.cloned.1.call-done = bf16[16,4,8192]{2,1,0:T(4,128)(2,1)} async-done(((bf16[1,4,8192]{2,1,0:T(4,128)(2,1)}), bf16[16,4,8192]{2,1,0:T(4,128)(2,1)}) %all-gather.8.cloned.1.call-update) | async-done | bytes 1048592 | tf_op jit(solution)/shard_map/all_gather | solution.py:65
  53.5 2.1 reshape.155
  55.7 0.0 all-gather.6.cloned.1.call-update
  55.7 0.0 copy-start.11
  55.7 0.0 copy-start.6
  55.7 0.0 copy-start.7
  55.7 0.0 copy-start.1
  55.8 4.7 all-to-all-start
  60.4 0.0 all-reduce.8.cloned.1.call-start
  60.5 0.0 copy-done.11
  60.5 0.2 reduce-window.8
  60.7 0.1 convert_reduce_fusion
  60.8 0.0 copy-done.6
  60.8 0.1 select_reduce_fusion.3
  60.9 0.0 copy-done.7
  60.9 0.1 select_reduce_fusion.1
  61.0 0.1 fusion.5
  61.1 0.0 copy-done.1
  61.1 2.1 fusion.8
  63.2 2.1 fusion.9
  65.3 0.1 copy.29
  65.5 90.2 %psum.7 = bf16[64,32]{0,1:T(8,128)(2,1)S(1)} all-reduce(f32[64,32]{0,1:T(8,128)S(1)} %bitcast.47), channel_id=1, replica_groups=mesh['tensor'=8,'adapter'=16] {'adapter'}, use_global_device_ids=true, to_apply=%region_5.6 | all-reduce | flops 2048 | bytes 12288 | tf_op jit(solution)/shard_map/psum | solution.py:70
  155.6 28.5 %all-gather.1 = bf16[8,64,32]{1,2,0:T(8,128)(2,1)S(1)} all-gather(bf16[1,64,32]{1,2,0:T(8,128)(2,1)S(1)} %bitcast.50), channel_id=1, replica_groups=mesh['tensor'=8,'adapter'=16] {'tensor'}, dimensions={0}, use_global_device_ids=true | all-gather | bytes 36864 | tf_op jit(solution)/shard_map/all_gather | solution.py:73
  184.2 0.1 reshape.157
  184.3 2.4 broadcast_select_fusion.1
  186.7 0.0 copy-start.4
  186.7 0.0 all-gather.6.cloned.1.call-done
  186.7 0.0 copy-start.2
  186.7 7.2 %fusion.7 = f32[512,224]{0,1:T(8,128)S(1)} fusion(bf16[512,8192]{1,0:T(8,128)(2,1)} %all-gather.6.cloned.1.call-done, bf16[8192,224]{0,1:T(8,128)(2,1)} %param.14), kind=kOutput, calls=%fused_computation.31 | convolution fusion | flops 1879048192 | bytes 12517376 | tf_op jit(solution)/shard_map/dot_general | solution.py:75
  194.0 0.0 copy-start.9
  194.0 0.0 copy-done.4
  194.0 0.0 copy-done.2
  194.0 0.6 convolution_add_fusion.1
  194.7 0.0 copy-done.8
  194.7 1.5 copy-done.9
  196.2 2.7 fusion.10
  198.8 0.0 copy-start.5
  198.9 0.0 copy-done.3
  198.9 0.0 copy-done.10
  198.9 0.7 fusion.1
  199.5 0.5 copy-done.5
  200.0 0.8 fusion.12
  200.8 0.9 select_reduce_fusion
  201.6 0.1 copy.33
  201.8 65.0 %all-reduce.1 = bf16[512,16]{1,0:T(8,128)(2,1)S(1)} all-reduce(f32[512,16]{1,0:T(8,128)S(1)} %copy.33), channel_id=3, replica_groups=mesh['tensor'=8,'adapter'=16] {'tensor','adapter'}, use_global_device_ids=true, to_apply=%region_8.9.clone | all-reduce | flops 8192 | bytes 49152
  266.8 16.0 %all-gather.2 = bf16[16,4,16]{2,1,0:T(4,128)(2,1)S(1)} all-gather(bf16[1,4,16]{2,1,0:T(4,128)(2,1)S(1)} %fusion.4), channel_id=1, replica_groups=mesh['tensor'=8,'adapter'=16] {'adapter'}, dimensions={0}, use_global_device_ids=true | all-gather | bytes 2176 | tf_op jit(solution)/shard_map/all_gather | solution.py:93
  282.8 0.1 copy.34
  282.9 0.0 copy-done
  282.9 1.5 convolution_convert_fusion
  284.4 0.0 all-reduce.8.cloned.1.call-update
  284.4 0.0 all-reduce.6.cloned.1.call-start
  284.4 0.0 all-to-all-done
  284.4 2.4 copy.36
  286.9 8.1 %fusion.11 = f32[512,8192]{1,0:T(8,128)} fusion(bf16[512,224]{0,1:T(8,128)(2,1)S(1)} %fusion.1, bf16[224,8192]{1,0:T(8,128)(2,1)S(1)} %bitcast.41), kind=kOutput, calls=%fused_computation.35 | convolution fusion | flops 1879048192 | bytes 20676608 | tf_op jit(solution)/shard_map/dot_general | solution.py:87
  295.0 0.0 all-reduce.6.cloned.1.call-update
  295.0 0.6 copy-done.12
  295.6 0.6 dynamic-slice.2
  296.9 76.9 %all-reduce.8.cloned.1.call-done = bf16[64,8192]{1,0:T(8,128)(2,1)} async-done(((bf16[64,8192]{1,0:T(8,128)(2,1)}), bf16[64,8192]{1,0:T(8,128)(2,1)}) %all-reduce.8.cloned.1.call-update) | async-done | bytes 1048592
  373.8 222.0 %all-reduce.6.cloned.1.call-done = f32[512,8192]{1,0:T(8,128)} async-done(((f32[512,8192]{1,0:T(8,128)}), f32[512,8192]{1,0:T(8,128)}) %all-reduce.6.cloned.1.call-update) | async-done | bytes 16777232
  595.9 1.7 fusion.2
  (13 shorter events, 0.2 us)
Async XLA Ops:
  6.5 276.3 %copy-start = (bf16[128,8192]{1,0:T(8,128)(2,1)S(1)}, bf16[128,8192]{1,0:T(8,128)(2,1)}, u32[]{:S(2)}) copy-start(bf16[128,8192]{1,0:T(8,128)(2,1)} %param.22) | copy-start | bytes 6291460
  6.5 47.0 %all-gather.8.cloned.1.call-start = ((), (), s32[]{:S(2)}) async-start(), calls=%async_computation.2 | async-start | bytes 1114112 | tf_op jit(solution)/shard_map/all_gather | solution.py:65
  7.3 179.5 %all-gather.6.cloned.1.call-start = ((), (), s32[]{:S(2)}) async-start(), calls=%async_computation.1 | async-start | bytes 9437184 | tf_op jit(solution)/shard_map/all_gather | solution.py:72
  55.7 4.8 copy-start.11
  55.7 5.0 copy-start.6
  55.7 5.1 copy-start.7
  55.7 5.4 copy-start.1
  55.8 228.7 %all-to-all-start = ((bf16[16,224,512]{2,1,0:T(8,128)(2,1)}), bf16[16,224,512]{2,1,0:T(8,128)(2,1)}, u32[]{:S(2)}, u32[]{:S(2)}) async-start(bf16[16,224,512]{2,1,0:T(8,128)(2,1)} %bitcast.43), calls=%async_computation | async-start | bytes 7340032 | tf_op jit(solution)/shard_map/all_to_all | solution.py:86
  60.4 313.4 %all-reduce.8.cloned.1.call-start = ((), (), s32[]{:S(2)}) async-start(), calls=%async_computation.4 | async-start | bytes 2097152
  186.7 7.3 %copy-start.4 = (bf16[2048,224]{0,1:T(8,128)(2,1)S(1)}, bf16[2048,224]{0,1:T(8,128)(2,1)}, u32[]{:S(2)}) copy-start(bf16[2048,224]{0,1:T(8,128)(2,1)} %param.19) | copy-start | bytes 2752516
  186.7 7.3 %copy-start.2 = (bf16[512,128,16]{0,2,1:T(8,128)(2,1)S(1)}, bf16[512,128,16]{0,2,1:T(8,128)(2,1)}, u32[]{:S(2)}) copy-start(bf16[512,128,16]{0,2,1:T(8,128)(2,1)} %get-tuple-element.7) | copy-start | bytes 6291460
  186.7 7.9 %copy-start.8 = (bf16[512,8192]{1,0:T(8,128)(2,1)S(1)}, bf16[512,8192]{1,0:T(8,128)(2,1)}, u32[]{:S(2)}) copy-start(bf16[512,8192]{1,0:T(8,128)(2,1)} %all-gather.6.cloned.1.call-done) | copy-start | bytes 25165828
  194.0 2.2 copy-start.9
  196.2 2.7 copy-start.3
  196.2 2.7 copy-start.10
  198.8 1.2 copy-start.5
  284.4 311.5 %all-reduce.6.cloned.1.call-start = ((), (), s32[]{:S(2)}) async-start(), calls=%async_computation.3 | async-start | bytes 33554432
  295.0 0.7 copy-start.12
Sparse Core Ops, SparseCore 0:
  9.5 44.0 all-gather.7
  55.8 51.1 all-gather.5
  284.5 89.2 all-reduce.7
  379.1 216.7 all-reduce.5
where the time goes:
time: 605 us; the launch traced here: 604 us
  waiting for transfers between devices  346 us (57%)
  blocking collectives  200 us (33%)
  matrix products  25.7 us (4%)
  between operations  14.1 us (2%)
  local copies, waits for them, and re-layouts  8.25 us (1%)
    unnamed x6, waiting for transfers between devices  300 us
    psum x1, blocking collectives, local(): shrunk_group = lax.psum(picked, 'adapter').astype(jnp.bfloat16)  90.2 us
    unnamed x1, blocking collectives  65 us
    all_gather x1, waiting for transfers between devices, local(): rows_group = lax.all_gather(tokens_in, 'adapter', axis=0, tiled=True)  46.2 us
    all_gather x1, blocking collectives, local(): lax.all_gather(shrunk_group, 'tensor', axis=0, tiled=True)  28.5 us
    all_gather x1, blocking collectives, local(): low_group = lax.all_gather(low_rank, 'adapter', axis=0, tiled=True)  16 us
  transfers between devices with their start and end apart: 5, of which 3 were waited for; matrix products, arithmetic and copies ran while one was open for 5% of the time, Pallas kernels for 0%

commit v1 on v0

--- a/solution.py
+++ b/solution.py
@@ -5,6 +5,27 @@
 
 R = 16
 ADP_DEV = 8
+
+
+def ring_gather(x, axis, dim):
+    count, index, width = (lax.axis_size(axis), lax.axis_index(axis), x.shape[dim])
+    ahead = [(i, (i + 1) % count) for i in range(count)]
+    behind = [(i, (i - 1) % count) for i in range(count)]
+    filled = jnp.zeros((*x.shape[:dim], count * width, *x.shape[dim + 1 :]), x.dtype)
+    filled = lax.dynamic_update_slice_in_dim(filled, x, index * width, axis=dim)
+    from_left = from_right = x
+    middle = count // 2
+    for step in range(1, middle + 1):
+        from_left = lax.ppermute(from_left, axis, ahead)
+        filled = lax.dynamic_update_slice_in_dim(
+            filled, from_left, (index - step) % count * width, axis=dim
+        )
+        if step < count - middle:
+            from_right = lax.ppermute(from_right, axis, behind)
+            filled = lax.dynamic_update_slice_in_dim(
+                filled, from_right, (index + step) % count * width, axis=dim
+            )
+    return filled
 
 
 def token_tables(lengths, request_adapter, placement, all_tokens):
@@ -70,7 +91,7 @@
     shrunk_group = lax.psum(picked, "adapter").astype(jnp.bfloat16)
     gathered, shrunk_all = (
         lax.all_gather(rows_group, "tensor", axis=0, tiled=True),
-        lax.all_gather(shrunk_group, "tensor", axis=0, tiled=True),
+        ring_gather(shrunk_group, "tensor", 0),
     )
     gate_sum = jnp.dot(gathered, w_gate, preferred_element_type=jnp.float32) + jnp.dot(
         spread_block(shrunk_all[:, :R], adapter_hot), b_gate, preferred_element_type=jnp.float32

time: 605 us -> 594 us (0.982)
  blocking collectives: 200 us -> 158 us
  starting transfers between devices: 4.78 us -> 28.2 us
    psum x1, blocking collectives: 90.2 us -> 57.9 us  [local(): shrunk_group = lax.psum(picked, 'adapter').astype(jnp.bfloat16)]
    all_gather x1 -> x0, blocking collectives: 28.5 us -> none  [local(): lax.all_gather(shrunk_group, 'tensor', axis=0, tiled=True)]
    ppermute x0 -> x7, starting transfers between devices: none -> 23.5 us  [the longest x4 22.4 us: ring_gather(): from_left = lax.ppermute(from_left, axis, ahead)]
    unnamed x1, blocking collectives: 65 us -> 83.3 us
  transfers between devices with their start and end apart: 5 -> 12, of which waited for: 3 -> 7; matrix products, arithmetic and copies ran while one was open for 5% -> 6% of each run, Pallas kernels for 0% -> 0%
where the time goes in v1:
time: 594 us; the launch traced here: 593 us
  waiting for transfers between devices  349 us (59%)
  blocking collectives  158 us (27%)
  starting transfers between devices  28.2 us (5%)
  matrix products  26.1 us (4%)
  between operations  14.1 us (2%)
  local copies, waits for them, and re-layouts  9.88 us (2%)
  other arithmetic  7.63 us (1%)
    unnamed x6, waiting for transfers between devices  299 us
    unnamed x1, blocking collectives  83.3 us
    psum x1, blocking collectives, local(): shrunk_group = lax.psum(picked, 'adapter').astype(jnp.bfloat16)  57.9 us
    all_gather x1, waiting for transfers between devices, local(): rows_group = lax.all_gather(tokens_in, 'adapter', axis=0, tiled=True)  46.2 us
    ppermute x4, starting transfers between devices, ring_gather(): from_left = lax.ppermute(from_left, axis, ahead)  22.4 us
    all_gather x1, blocking collectives, local(): low_group = lax.all_gather(low_rank, 'adapter', axis=0, tiled=True)  17.2 us
  transfers between devices with their start and end apart: 12, of which 7 were waited for; matrix products, arithmetic and copies ran while one was open for 6% of the time, Pallas kernels for 0%

profile of v1, /device:TPU:1, one launch (start us, length us, event | category | flops | bytes accessed | tf_op | source)
XLA Modules:
  0.0 593.3 jit_solution(7147196665726780806)
XLA Ops:
  6.5 0.7 all-gather.7.cloned.1.call-update
  7.3 0.0 all-gather.5.cloned.1.call-start
  7.3 46.2 %all-gather.7.cloned.1.call-done = bf16[16,4,8192]{2,1,0:T(4,128)(2,1)} async-done(((bf16[1,4,8192]{2,1,0:T(4,128)(2,1)}), bf16[16,4,8192]{2,1,0:T(4,128)(2,1)}) %all-gather.7.cloned.1.call-update) | async-done | bytes 1048592 | tf_op jit(solution)/shard_map/all_gather | solution.py:86
  53.5 2.1 reshape.155
  55.7 0.0 all-gather.5.cloned.1.call-update
  55.7 0.9 reduce-window.8
  56.6 0.1 convert_reduce_fusion
  56.7 0.7 select_reduce_fusion.3
  57.5 0.8 select_reduce_fusion.1
  58.2 0.1 fusion.5
  58.3 2.4 fusion.8
  60.8 2.1 fusion.9
  62.9 0.1 copy.23
  63.0 57.9 %psum.7 = bf16[64,32]{0,1:T(8,128)(2,1)S(1)} all-reduce(f32[64,32]{0,1:T(8,128)S(1)} %bitcast.42), channel_id=1, replica_groups=mesh['tensor'=8,'adapter'=16] {'adapter'}, use_global_device_ids=true, to_apply=%region_5.6 | all-reduce | flops 2048 | bytes 12288 | tf_op jit(solution)/shard_map/psum | solution.py:91
  120.8 17.8 %collective-permute-start = (bf16[64,32]{0,1:T(8,128)(2,1)S(1)}, bf16[64,32]{0,1:T(8,128)(2,1)S(1)}, u32[]{:S(2)}, u32[]{:S(2)}) collective-permute-start(bf16[64,32]{0,1:T(8,128)(2,1)S(1)} %psum.7), channel_id=1, source_target_pairs={{0,16},{16,32},{32,48},{48,64},{64,80},{80,96},{96,112},{112,0},{1... | collective-permute-start | bytes 12296 | tf_op jit(solution)/shard_map/ppermute | solution.py:19
  138.6 0.0 collective-permute-start.1
  138.6 0.8 collective-permute-done
  139.4 2.3 collective-permute-start.2
  141.7 4.5 all-to-all-start
  146.2 0.0 all-reduce.8.cloned.1.call-start
  146.3 0.0 collective-permute-done.1
  146.3 0.1 collective-permute-start.3
  146.4 0.0 collective-permute-done.2
  146.4 1.6 collective-permute-start.4
  148.1 1.6 collective-permute-done.3
  149.8 1.0 collective-permute-start.5
  150.7 0.8 collective-permute-start.6
  151.5 0.3 dynamic_update_slice.24
  151.8 0.2 dynamic_update_slice.25
  152.0 0.2 dynamic_update_slice.26
  152.2 0.3 dynamic_update_slice.27
  152.5 0.3 dynamic_update_slice.28
  152.8 0.2 dynamic_update_slice.29
  153.0 0.3 collective-permute-done.5
  153.2 0.1 dynamic_update_slice.30
  153.4 1.4 collective-permute-done.6
  154.7 0.3 dynamic_update_slice.31
  155.0 2.4 broadcast_select_fusion.1
  157.4 7.3 %fusion.7 = f32[512,224]{0,1:T(8,128)S(1)} fusion(bf16[512,8192]{1,0:T(8,128)(2,1)} %all-gather.5.cloned.1.call-done, bf16[8192,224]{0,1:T(8,128)(2,1)} %param.14), kind=kOutput, calls=%fused_computation.30 | convolution fusion | flops 1879048192 | bytes 12517376 | tf_op jit(solution)/shard_map/dot_general | solution.py:96
  164.7 0.0 copy-start.7
  164.7 0.6 convolution_add_fusion.1
  165.4 1.5 copy-done.7
  166.9 2.7 fusion.10
  169.5 0.0 copy-start.5
  169.6 0.7 fusion.1
  170.2 0.5 copy-done.5
  170.7 0.8 fusion.12
  171.5 0.9 select_reduce_fusion
  172.4 0.1 copy.26
  172.5 83.3 %all-reduce.1 = bf16[512,16]{1,0:T(8,128)(2,1)S(1)} all-reduce(f32[512,16]{1,0:T(8,128)S(1)} %copy.26), channel_id=3, replica_groups=mesh['tensor'=8,'adapter'=16] {'tensor','adapter'}, use_global_device_ids=true, to_apply=%region_8.9.clone | all-reduce | flops 8192 | bytes 49152
  255.8 17.2 %all-gather.1 = bf16[16,4,16]{2,1,0:T(4,128)(2,1)S(1)} all-gather(bf16[1,4,16]{2,1,0:T(4,128)(2,1)S(1)} %fusion.4), channel_id=1, replica_groups=mesh['tensor'=8,'adapter'=16] {'adapter'}, dimensions={0}, use_global_device_ids=true | all-gather | bytes 2176 | tf_op jit(solution)/shard_map/all_gather | solution.py:114
  273.0 0.1 copy.27
  273.1 1.5 convolution_convert_fusion
  274.6 0.0 all-reduce.8.cloned.1.call-update
  274.6 0.0 all-reduce.6.cloned.1.call-start
  274.7 0.0 all-to-all-done
  274.7 2.4 copy.29
  277.1 8.1 %fusion.11 = f32[512,8192]{1,0:T(8,128)} fusion(bf16[512,224]{0,1:T(8,128)(2,1)S(1)} %fusion.1, bf16[224,8192]{1,0:T(8,128)(2,1)S(1)} %bitcast.36), kind=kOutput, calls=%fused_computation.34 | convolution fusion | flops 1879048192 | bytes 20676608 | tf_op jit(solution)/shard_map/dot_general | solution.py:108
  285.2 0.0 all-reduce.6.cloned.1.call-update
  285.3 0.6 copy-done.9
  285.9 0.6 dynamic-slice.2
  287.1 75.9 %all-reduce.8.cloned.1.call-done = bf16[64,8192]{1,0:T(8,128)(2,1)} async-done(((bf16[64,8192]{1,0:T(8,128)(2,1)}), bf16[64,8192]{1,0:T(8,128)(2,1)}) %all-reduce.8.cloned.1.call-update) | async-done | bytes 1048592
  363.1 222.0 %all-reduce.6.cloned.1.call-done = f32[512,8192]{1,0:T(8,128)} async-done(((f32[512,8192]{1,0:T(8,128)}), f32[512,8192]{1,0:T(8,128)}) %all-reduce.6.cloned.1.call-update) | async-done | bytes 16777232
  585.1 1.7 fusion.2
  (27 shorter events, 0.2 us)
Async XLA Ops:
  6.5 266.6 %copy-start = (bf16[128,8192]{1,0:T(8,128)(2,1)S(1)}, bf16[128,8192]{1,0:T(8,128)(2,1)}, u32[]{:S(2)}) copy-start(bf16[128,8192]{1,0:T(8,128)(2,1)} %param.22) | copy-start | bytes 6291460
  6.5 47.0 %all-gather.7.cloned.1.call-start = ((), (), s32[]{:S(2)}) async-start(), calls=%async_computation.2 | async-start | bytes 1114112 | tf_op jit(solution)/shard_map/all_gather | solution.py:86
  7.3 150.2 %all-gather.5.cloned.1.call-start = ((), (), s32[]{:S(2)}) async-start(), calls=%async_computation.1 | async-start | bytes 9437184 | tf_op jit(solution)/shard_map/all_gather | solution.py:93
  55.7 5.1 copy-start.1
  120.8 18.6 %collective-permute-start = (bf16[64,32]{0,1:T(8,128)(2,1)S(1)}, bf16[64,32]{0,1:T(8,128)(2,1)S(1)}, u32[]{:S(2)}, u32[]{:S(2)}) collective-permute-start(bf16[64,32]{0,1:T(8,128)(2,1)S(1)} %psum.7), channel_id=1, source_target_pairs={{0,16},{16,32},{32,48},{48,64},{64,80},{80,96},{96,112},{112,0},{1... | collective-permute-start | bytes 12296 | tf_op jit(solution)/shard_map/ppermute | solution.py:19
  138.6 7.7 %collective-permute-start.1 = (bf16[64,32]{0,1:T(8,128)(2,1)S(1)}, bf16[64,32]{0,1:T(8,128)(2,1)S(1)}, u32[]{:S(2)}, u32[]{:S(2)}) collective-permute-start(bf16[64,32]{0,1:T(8,128)(2,1)S(1)} %psum.7), channel_id=1, source_target_pairs={{0,112},{16,0},{32,16},{48,32},{64,48},{80,64},{96,80},{112,96},{1... | collective-permute-start | bytes 12296 | tf_op jit(solution)/shard_map/ppermute | solution.py:24
  139.4 7.0 %collective-permute-start.2 = (bf16[64,32]{0,1:T(8,128)(2,1)S(1)}, bf16[64,32]{0,1:T(8,128)(2,1)S(1)}, u32[]{:S(2)}, u32[]{:S(2)}) collective-permute-start(bf16[64,32]{0,1:T(8,128)(2,1)S(1)} %collective-permute-done), channel_id=1, source_target_pairs={{0,16},{16,32},{32,48},{48,64},{64,80},{80,96},{96,112},{112,0},{1... | collective-permute-start | bytes 12296 | tf_op jit(solution)/shard_map/ppermute | solution.py:19
  141.7 133.0 %all-to-all-start = ((bf16[16,224,512]{2,1,0:T(8,128)(2,1)}), bf16[16,224,512]{2,1,0:T(8,128)(2,1)}, u32[]{:S(2)}, u32[]{:S(2)}) async-start(bf16[16,224,512]{2,1,0:T(8,128)(2,1)} %bitcast.38), calls=%async_computation | async-start | bytes 7340032 | tf_op jit(solution)/shard_map/all_to_all | solution.py:107
  146.2 216.9 %all-reduce.8.cloned.1.call-start = ((), (), s32[]{:S(2)}) async-start(), calls=%async_computation.4 | async-start | bytes 2097152
  146.3 3.5 collective-permute-start.3
  146.4 4.3 collective-permute-start.4
  149.8 3.5 collective-permute-start.5
  150.7 4.0 collective-permute-start.6
  157.4 7.3 %copy-start.4 = (bf16[2048,224]{0,1:T(8,128)(2,1)S(1)}, bf16[2048,224]{0,1:T(8,128)(2,1)}, u32[]{:S(2)}) copy-start(bf16[2048,224]{0,1:T(8,128)(2,1)} %param.19) | copy-start | bytes 2752516
  157.4 7.3 %copy-start.2 = (bf16[512,128,16]{0,2,1:T(8,128)(2,1)S(1)}, bf16[512,128,16]{0,2,1:T(8,128)(2,1)}, u32[]{:S(2)}) copy-start(bf16[512,128,16]{0,2,1:T(8,128)(2,1)} %get-tuple-element.7) | copy-start | bytes 6291460
  157.4 8.0 %copy-start.6 = (bf16[512,8192]{1,0:T(8,128)(2,1)S(1)}, bf16[512,8192]{1,0:T(8,128)(2,1)}, u32[]{:S(2)}) copy-start(bf16[512,8192]{1,0:T(8,128)(2,1)} %all-gather.5.cloned.1.call-done) | copy-start | bytes 25165828
  164.7 2.2 copy-start.7
  166.9 2.7 copy-start.3
  166.9 2.7 copy-start.8
  169.5 1.2 copy-start.5
  274.6 310.5 %all-reduce.6.cloned.1.call-start = ((), (), s32[]{:S(2)}) async-start(), calls=%async_computation.3 | async-start | bytes 33554432
  285.2 0.7 copy-start.9
Sparse Core Ops, SparseCore 0:
  9.5 44.0 all-gather.6
  55.8 51.1 all-gather.4
  274.7 88.2 all-reduce.7
  368.4 216.7 all-reduce.5
